TPU v7x, 32 devices: a whole 2x2x4 slice. The times are simulated.
32 devices in a mesh: row: 4 (over x, core), col: 8 (over z, y).
Axes of the slice: x: 2, y: 2, z: 4, core: 2. Of those that a mesh axis runs over, the one named last changes fastest.
Arguments:
- corner: bfloat16 [25600, 25600], P('row', 'col'), may hold values from -32 to 32
- edge: bfloat16 [25600, 25600], P('row', 'col'), may hold values from -32 to 32
- sketch: bfloat16 [25600, 448], P('col'), may hold values from -6 to 6
Outputs:
- corner_new: float32 [400, 400], replicated
- edge_new: float32 [400, 400], replicated
All inputs are finite; a program needn't handle non-finite values.
Results may differ from a plain program's by a relative error of at most 0.0015.
Values may be sent and summed in bfloat16 or wider, within the bound.
A program may use at most 256 MiB of HBM per device.

v0:
```python
import functools

import jax
import jax.numpy as jnp
from jax import lax
from jax.experimental import pallas as pl
from jax.experimental.pallas import tpu as pltpu
from jax.sharding import PartitionSpec as P

RANK = 400
HIGHEST = lax.Precision.HIGHEST
BLOCK = 128
TILE = 8
VMEM_LIMIT = 58 * 1024 * 1024


def outer(left, right, precision=None):
    return lax.dot_general(
        left, right, (((0,), (0,)), ((), ())), precision=precision, preferred_element_type=jnp.float32
    )


def row_tile(rows):
    for tile in (640, 512, 400, 320, 256, 160, 128, 64, 32, 16):
        if rows % tile == 0:
            return tile
    return rows


def sample_kernel(matrix, sketch, out):
    out[...] = jnp.dot(matrix[...], sketch[...], preferred_element_type=jnp.float32).astype(out.dtype)


def sample(matrix, sketch):
    rows, depth = matrix.shape
    width = sketch.shape[1]
    tile = row_tile(rows)
    return pl.pallas_call(
        sample_kernel,
        grid=(rows // tile,),
        out_shape=jax.ShapeDtypeStruct((rows, width), jnp.bfloat16),
        in_specs=[
            pl.BlockSpec((tile, depth), lambda i: (i, 0)),
            pl.BlockSpec((depth, width), lambda i: (0, 0)),
        ],
        out_specs=pl.BlockSpec((tile, width), lambda i: (i, 0)),
        compiler_params=pltpu.CompilerParams(vmem_limit_bytes=VMEM_LIMIT),
    )(matrix, sketch)


def image_kernel(matrix, cols, out):
    out[...] = jnp.dot(matrix[...], cols[...], preferred_element_type=jnp.float32)


def image_of(matrix, cols):
    height, depth = matrix.shape
    width = cols.shape[1]
    tile = row_tile(height)
    return pl.pallas_call(
        image_kernel,
        grid=(height // tile,),
        out_shape=jax.ShapeDtypeStruct((height, width), jnp.float32),
        in_specs=[
            pl.BlockSpec((tile, depth), lambda i: (i, 0)),
            pl.BlockSpec((depth, width), lambda i: (0, 0)),
        ],
        out_specs=pl.BlockSpec((tile, width), lambda i: (i, 0)),
        cost_estimate=pl.CostEstimate(
            flops=2 * height * depth * width, bytes_accessed=2 * height * depth, transcendentals=0
        ),
        compiler_params=pltpu.CompilerParams(vmem_limit_bytes=VMEM_LIMIT),
    )(matrix, cols)


def left_kernel(rows, first, second, first_out, second_out):
    left = rows[...].T

    def term(image):
        upper_part = image.astype(jnp.bfloat16)
        lower_part = (image - upper_part.astype(jnp.float32)).astype(jnp.bfloat16)
        found = jnp.dot(left, upper_part, preferred_element_type=jnp.float32)
        return found + jnp.dot(left, lower_part, preferred_element_type=jnp.float32)

    @pl.when(pl.program_id(0) == 0)
    def _():
        first_out[...] = jnp.zeros_like(first_out)
        second_out[...] = jnp.zeros_like(second_out)

    first_out[...] += term(first[...])
    second_out[...] += term(second[...])


def left_products(rows, first, second):
    height, width = rows.shape
    tile = row_tile(height)
    tall = pl.BlockSpec((tile, width), lambda i: (i, 0))
    square = pl.BlockSpec((width, width), lambda i: (0, 0))
    shape = jax.ShapeDtypeStruct((width, width), jnp.float32)
    return pl.pallas_call(
        left_kernel,
        grid=(height // tile,),
        out_shape=(shape, shape),
        in_specs=[tall, tall, tall],
        out_specs=(square, square),
        compiler_params=pltpu.CompilerParams(vmem_limit_bytes=VMEM_LIMIT),
    )(rows, first, second)


def eliminate(block):
    count = block.shape[0] // TILE
    row_ids = lax.broadcasted_iota(jnp.int32, (TILE, BLOCK), 0)
    lane_ids = lax.broadcasted_iota(jnp.int32, (TILE, BLOCK), 1)
    work = [block[t * TILE : (t + 1) * TILE, :] for t in range(count)]
    other = [(lane_ids == row_ids + t * TILE).astype(jnp.float32) for t in range(count)]
    for step in range(count * TILE):
        home, place = divmod(step, TILE)
        column = [jnp.broadcast_to(work[t][:, step : step + 1], (TILE, BLOCK)) for t in range(home, count)]
        scale = 1.0 / column[0][place : place + 1, :]
        pivot_row = work[home][place : place + 1, :] * scale
        other_row = other[home][place : place + 1, :] * scale
        for t in range(home, count):
            factor = column[t - home]
            if t == home:
                factor = jnp.where(row_ids > place, factor, 0.0)
            work[t] = work[t] - factor * pivot_row
            other[t] = other[t] - factor * other_row
    done = []
    for t in range(count):
        diagonal = jnp.sum(jnp.where(lane_ids == row_ids + t * TILE, work[t], 0.0), axis=1, keepdims=True)
        done.append(other[t] / jnp.sqrt(diagonal))
    return jnp.concatenate(done, axis=0)


def factor_kernel(gram, out, held):
    size = gram.shape[0]
    padded = held.shape[0]
    ids_r = lax.broadcasted_iota(jnp.int32, (padded, padded), 0)
    ids_c = lax.broadcasted_iota(jnp.int32, (padded, padded), 1)
    unit = (ids_r == ids_c).astype(jnp.float32)
    held[:, :padded] = unit
    held[:, padded:] = unit
    held[:size, :size] = gram[...]
    blocks = padded // BLOCK

    def one(k, carry):
        at = pl.multiple_of(k * BLOCK, BLOCK)
        inverse = eliminate(held[pl.ds(at, BLOCK), pl.ds(at, BLOCK)])
        strip = jnp.dot(inverse, held[pl.ds(at, BLOCK), :], precision=HIGHEST, preferred_element_type=jnp.float32)
        held[pl.ds(at, BLOCK), :] = strip

        def trail(i, inner):
            low = pl.multiple_of(i * BLOCK, BLOCK)
            side = held[pl.ds(at, BLOCK), pl.ds(low, BLOCK)]
            held[pl.ds(low, BLOCK), :] -= jnp.dot(
                side.T, held[pl.ds(at, BLOCK), :], precision=HIGHEST, preferred_element_type=jnp.float32
            )
            return inner

        lax.fori_loop(k + 1, blocks, trail, 0)
        return carry

    lax.fori_loop(0, blocks, one, 0)
    out[...] = held[:size, padded : padded + size]


def inverse_factor(gram):
    size = gram.shape[0]
    padded = -(-size // BLOCK) * BLOCK
    whole = pl.pallas_call(
        factor_kernel,
        out_shape=jax.ShapeDtypeStruct((size, size), jnp.float32),
        in_specs=[pl.BlockSpec(memory_space=pltpu.VMEM)],
        out_specs=pl.BlockSpec(memory_space=pltpu.VMEM),
        scratch_shapes=[pltpu.VMEM((padded, 2 * padded), jnp.float32)],
        cost_estimate=pl.CostEstimate(
            flops=100 * padded * padded * padded, bytes_accessed=8 * size * size, transcendentals=0
        ),
    )(gram)
    return whole[size - RANK :]


def reduce_kernel(n_row, n_col, x, out, row_land, col_land, part, total, *sems):
    send_a, recv_a, send_b, recv_b, send_c, recv_c, send_d, recv_d = sems
    me_row, me_col = lax.axis_index("row"), lax.axis_index("col")
    big = x.shape[0] // n_row
    small = big // n_col

    def peer(me, shift, count):
        return lax.rem(me + shift, count)

    def row_of(shift):
        return (peer(me_row, shift, n_row), me_col)

    def col_of(shift):
        return (me_row, peer(me_col, shift, n_col))

    def copy(source, target, send, recv, device):
        return pltpu.make_async_remote_copy(
            src_ref=source, dst_ref=target, send_sem=send, recv_sem=recv,
            device_id=device, device_id_type=pl.DeviceIdType.MESH,
        )

    def at(index, size):
        return pl.ds(pl.multiple_of(index * size, TILE), size)

    barrier = pltpu.get_barrier_semaphore()
    for d in range(1, n_row):
        pl.semaphore_signal(barrier, inc=1, device_id=row_of(d), device_id_type=pl.DeviceIdType.MESH)
    for d in range(1, n_col):
        pl.semaphore_signal(barrier, inc=1, device_id=col_of(d), device_id_type=pl.DeviceIdType.MESH)
    pl.semaphore_wait(barrier, n_row + n_col - 2)

    first = []
    for d in range(1, n_row):
        chunk = x.at[at(peer(me_row, d, n_row), big), :]
        first.append(copy(chunk, row_land.at[d - 1], send_a.at[d - 1], recv_a.at[d - 1], row_of(d)))
        first[-1].start()
    summed = x[at(me_row, big), :]
    for d in range(1, n_row):
        first[d - 1].wait_recv()
        summed += row_land[d - 1]
    part[...] = summed

    second = []
    for d in range(1, n_col):
        chunk = part.at[at(peer(me_col, d, n_col), small), :]
        second.append(copy(chunk, col_land.at[d - 1], send_b.at[d - 1], recv_b.at[d - 1], col_of(d)))
        second[-1].start()
    summed = part[at(me_col, small), :]
    for d in range(1, n_col):
        second[d - 1].wait_recv()
        summed += col_land[d - 1]
    total[...] = summed

    mine = pl.ds(pl.multiple_of(me_row * big + me_col * small, TILE), small)
    third = []
    for d in range(1, n_col):
        third.append(copy(total, out.at[mine, :], send_c.at[d - 1], recv_c.at[d - 1], col_of(d)))
        third[-1].start()
    out[mine, :] = summed
    for d in range(1, n_col):
        third[d - 1].wait_recv()

    fourth = []
    for d in range(1, n_row):
        chunk = out.at[at(me_row, big), :]
        fourth.append(copy(chunk, chunk, send_d.at[d - 1], recv_d.at[d - 1], row_of(d)))
        fourth[-1].start()
    for d in range(1, n_row):
        fourth[d - 1].wait_recv()
    for sent in first + second + third + fourth:
        sent.wait_send()


def reduce_all(value, collective_id):
    n_row, n_col = lax.axis_size("row"), lax.axis_size("col")
    height, width = value.shape
    grain = n_row * n_col * TILE
    padded = -(-height // grain) * grain
    value = jnp.pad(value, ((0, padded - height), (0, 0)))
    big = padded // n_row
    small = big // n_col
    dma = pltpu.SemaphoreType.DMA
    result = pl.pallas_call(
        functools.partial(reduce_kernel, n_row, n_col),
        out_shape=jax.ShapeDtypeStruct((padded, width), jnp.float32),
        in_specs=[pl.BlockSpec(memory_space=pltpu.VMEM)],
        out_specs=pl.BlockSpec(memory_space=pltpu.VMEM),
        scratch_shapes=[
            pltpu.VMEM((n_row - 1, big, width), jnp.float32),
            pltpu.VMEM((n_col - 1, small, width), jnp.float32),
            pltpu.VMEM((big, width), jnp.float32),
            pltpu.VMEM((small, width), jnp.float32),
        ]
        + [dma((n_row - 1,)), dma((n_row - 1,)), dma((n_col - 1,)), dma((n_col - 1,))]
        + [dma((n_col - 1,)), dma((n_col - 1,)), dma((n_row - 1,)), dma((n_row - 1,))],
        compiler_params=pltpu.CompilerParams(collective_id=collective_id, has_side_effects=True),
    )(value)
    return result[:height]


def column_route(n_row, n_col):
    ratio = n_col // n_row
    route = []
    for source in range(n_row):
        for shard in range(n_col):
            half, target = divmod(shard, n_row)
            route.append((source * n_col + shard, target * n_col + source * ratio + half))
    return route


def body(corner, edge, sketch):
    n_row, n_col = lax.axis_size("row"), lax.axis_size("col")
    both = ("row", "col")
    shard = lax.psum_scatter(sample(corner, sketch), "col", scatter_dimension=0, tiled=True)
    gram = reduce_all(outer(shard, shard), 0)
    shard, gram = lax.optimization_barrier((shard, gram))
    moved = lax.ppermute(shard, both, column_route(n_row, n_col))
    cols = lax.all_gather(moved, "row", axis=0, tiled=True)
    rows = lax.all_gather(shard, "col", axis=0, tiled=True)
    inverse = inverse_factor(gram)
    corner_image, edge_image = image_of(corner, cols), image_of(edge, cols)

    def renormalize(total):
        half = jnp.dot(inverse, total, precision=HIGHEST)
        return lax.dot_general(half, inverse, (((1,), (1,)), ((), ())), precision=HIGHEST)

    corner_sum, edge_sum = left_products(rows, corner_image, edge_image)
    stacked = jnp.concatenate([renormalize(corner_sum), renormalize(edge_sum)], axis=0)
    result = reduce_all(stacked, 1)
    return result[:RANK], result[RANK:]


def solution(mesh):
    placed = (P("row", "col"), P("row", "col"), P("col", None))
    return jax.shard_map(body, mesh=mesh, in_specs=placed, out_specs=(P(), P()), check_vma=False)
```

profile of v0, /device:TPU:31, one launch (start us, length us, event | category | flops | bytes accessed | tf_op | source)
XLA Modules:
  0.0 494.6 jit_solution(5855081475643301872)
XLA Ops:
  7.2 0.0 reduce-scatter.2.cloned.1.call-start
  7.2 5.4 %copy.9.sketch = bf16[3200,448]{1,0:T(8,128)(2,1)} copy(bf16[3200,448]{0,1:T(8,128)(2,1)} %param.5) | data formatting | bytes 5734400 | tf_op args[2]
  12.7 27.8 %shard_map.50 = bf16[6400,448]{1,0:T(8,128)(2,1)} custom-call(bf16[6400,3200]{1,0:T(8,128)(2,1)} %matrix.4, bf16[3200,448]{1,0:T(8,128)(2,1)} %copy.9.sketch), custom_call_target="tpu_custom_call" | custom-call | tf_op jit(solution)/shard_map/pallas_call | solution.py:38
  40.5 0.0 reduce-scatter.2.cloned.1.call-update
  40.5 0.0 all-gather.7.cloned.1.call-start
  40.6 121.3 %reduce-scatter.2.cloned.1.call-done = bf16[800,448]{1,0:T(8,128)(2,1)} async-done(((bf16[6400,448]{1,0:T(8,128)(2,1)}), bf16[800,448]{1,0:T(8,128)(2,1)}) %reduce-scatter.2.cloned.1.call-update) | async-done | bytes 716816 | tf_op jit(solution)/shard_map/reduce_scatter | solution.py:295
  161.9 2.1 fusion.9
  164.0 0.0 copy-start.1
  164.0 1.1 pad.8.x
  165.1 41.0 %shard_map.51 = f32[512,448]{1,0:T(8,128)} custom-call(f32[512,448]{1,0:T(8,128)} %pad.8.x), custom_call_target="tpu_custom_call" | custom-call | tf_op jit(solution)/shard_map/pallas_call | solution.py:264
  206.1 2.2 slice.15.gram
  208.3 0.0 copy-done.1
  208.3 0.8 copy.13
  209.1 0.7 collective-permute-start
  209.8 0.0 collective-permute-done
  209.8 0.0 copy-start.3
  209.8 0.9 copy-done.3
  210.7 0.0 all-gather.7.cloned.1.call-update
  210.7 0.2 all-gather.5.cloned.1.call-start
  211.0 1.2 copy.11
  212.2 0.0 all-gather.5.cloned.1.call-update
  212.2 51.4 %shard_map.52 = f32[448,448]{1,0:T(8,128)} custom-call(f32[448,448]{1,0:T(8,128)} %slice.15.gram), custom_call_target="tpu_custom_call" | custom-call | flops 13421772800 | bytes 1605632 | tf_op jit(solution)/shard_map/pallas_call | solution.py:169
  263.6 12.1 %all-gather.7.cloned.1.call-done = bf16[4,800,448]{1,2,0:T(8,128)(2,1)} async-done(((bf16[1,800,448]{1,2,0:T(8,128)(2,1)}), bf16[4,800,448]{1,2,0:T(8,128)(2,1)}) %all-gather.7.cloned.1.call-update) | async-done | bytes 2867216 | tf_op jit(solution)/shard_map/all_gather | solution.py:299
  275.7 5.8 %copy.14 = bf16[4,800,448]{2,1,0:T(8,128)(2,1)} copy(bf16[4,800,448]{1,2,0:T(8,128)(2,1)} %all-gather.7.cloned.1.call-done) | data formatting | bytes 5734400 | tf_op jit(solution)/shard_map/all_gather | solution.py:299
  281.5 29.6 %shard_map.53.first = f32[6400,448]{1,0:T(8,128)} custom-call(bf16[6400,3200]{1,0:T(8,128)(2,1)} %matrix.4, bf16[3200,448]{1,0:T(8,128)(2,1)} %bitcast.11), custom_call_target="tpu_custom_call" | custom-call | flops 18350080000 | bytes 40960000 | tf_op jit(solution)/shard_map/pallas_call | solution.py:59
  311.1 29.8 %shard_map.54.second = f32[6400,448]{1,0:T(8,128)} custom-call(bf16[6400,3200]{1,0:T(8,128)(2,1)} %matrix.5, bf16[3200,448]{1,0:T(8,128)(2,1)} %bitcast.12), custom_call_target="tpu_custom_call" | custom-call | flops 18350080000 | bytes 40960000 | tf_op jit(solution)/shard_map/pallas_call | solution.py:59
  340.8 35.8 %all-gather.5.cloned.1.call-done = bf16[8,800,448]{1,2,0:T(8,128)(2,1)} async-done(((bf16[1,800,448]{1,2,0:T(8,128)(2,1)}), bf16[8,800,448]{1,2,0:T(8,128)(2,1)}) %all-gather.5.cloned.1.call-update) | async-done | bytes 5734416 | tf_op jit(solution)/shard_map/all_gather | solution.py:300
  376.6 11.0 %copy.12 = bf16[8,800,448]{2,1,0:T(8,128)(2,1)} copy(bf16[8,800,448]{1,2,0:T(8,128)(2,1)} %all-gather.5.cloned.1.call-done) | data formatting | bytes 11468800 | tf_op jit(solution)/shard_map/all_gather | solution.py:300
  387.6 0.0 copy-start
  387.7 21.9 %shard_map.55 = (f32[448,448]{1,0:T(8,128)}, f32[448,448]{1,0:T(8,128)}) custom-call(bf16[6400,448]{1,0:T(8,128)(2,1)} %bitcast.10, f32[6400,448]{1,0:T(8,128)} %shard_map.53.first, f32[6400,448]{1,0:T(8,128)} %shard_map.54.second), custom_call_target="tpu_custom_call" | custom-call | tf_op jit(solution)/shard_map/pallas_call | solution.py:99
  409.5 0.0 copy-start.2
  409.5 0.0 copy-done
  409.5 2.7 fusion.6
  412.3 1.5 fusion.4
  413.7 0.0 copy-done.2
  413.8 1.5 fusion.2
  415.3 1.5 fusion
  416.7 1.6 select_maximum_fusion.x
  418.3 67.1 %shard_map.56 = f32[1024,400]{1,0:T(8,128)} custom-call(f32[1024,400]{1,0:T(8,128)} %select_maximum_fusion.x), custom_call_target="tpu_custom_call" | custom-call | tf_op jit(solution)/shard_map/pallas_call | solution.py:264
  485.4 2.7 fusion.8
Async XLA Ops:
  7.2 154.7 %reduce-scatter.2.cloned.1.call-start = ((), (), s32[]{:S(2)}) async-start(), calls=%async_computation.1 | async-start | bytes 7372800 | tf_op jit(solution)/shard_map/reduce_scatter | solution.py:295
  40.5 235.2 %all-gather.7.cloned.1.call-start = ((), (), s32[]{:S(2)}) async-start(), calls=%async_computation.3 | async-start | bytes 4014080 | tf_op jit(solution)/shard_map/all_gather | solution.py:299
  164.0 44.3 %copy-start.1 = (bf16[800,448]{1,0:T(8,128)(2,1)S(1)}, bf16[800,448]{1,0:T(8,128)(2,1)}, u32[]{:S(2)}) copy-start(bf16[800,448]{1,0:T(8,128)(2,1)} %reduce-scatter.2.cloned.1.call-done) | copy-start | bytes 2150404
  209.1 0.7 collective-permute-start
  209.8 0.9 copy-start.3
  210.7 165.9 %all-gather.5.cloned.1.call-start = ((), (), s32[]{:S(2)}) async-start(), calls=%async_computation.2 | async-start | bytes 7225344 | tf_op jit(solution)/shard_map/all_gather | solution.py:300
  387.6 21.9 %copy-start = (f32[448,448]{1,0:T(8,128)S(1)}, f32[448,448]{1,0:T(8,128)}, u32[]{:S(2)}) copy-start(f32[448,448]{1,0:T(8,128)} %shard_map.52) | copy-start | bytes 2408452
  409.5 4.2 copy-start.2
Sparse Core Ops, SparseCore 0:
  40.6 121.2 reduce-scatter.1
  210.9 64.8 all-gather.6
  278.5 98.1 all-gather.4
where the time goes:
time: 497 us; the launch traced here: 495 us
  Pallas kernels  269 us (54%)
  waiting for transfers between devices  169 us (34%)
  local copies, waits for them, and re-layouts  31.2 us (6%)
  between operations  13.9 us (3%)
  matrix products  9.27 us (2%)
    reduce_scatter x1, waiting for transfers between devices, body(): lax.psum_scatter(sample(corner, sketch), 'col', scatter_dimension=0, tile...  121 us
    pallas_call x2, Pallas kernels, reduce_all(): pl.pallas_call(functools.partial(reduce_kernel, n_row, n_col), out_shape=...  108 us
    pallas_call x2, Pallas kernels, image_of(): pl.pallas_call(image_kernel, grid=(height // tile,), out_shape=jax.ShapeD...  59.4 us
    pallas_call x1, Pallas kernels, inverse_factor(): pl.pallas_call(factor_kernel, out_shape=jax.ShapeDtypeStruct((size, size)...  51.4 us
    all_gather x1, waiting for transfers between devices, body(): rows = lax.all_gather(shard, 'col', axis=0, tiled=True)  35.8 us
    pallas_call x1, Pallas kernels, sample(): pl.pallas_call(sample_kernel, grid=(rows // tile,), out_shape=jax.ShapeDt...  27.8 us
    pallas_call x1, Pallas kernels, left_products(): pl.pallas_call(left_kernel, grid=(height // tile,), out_shape=(shape, sha...  21.9 us
    all_gather x1, waiting for transfers between devices, body(): cols = lax.all_gather(moved, 'row', axis=0, tiled=True)  12.1 us
  transfers between devices with their start and end apart: 4, of which 3 were waited for; matrix products, arithmetic and copies ran while one was open for 1% of the time, Pallas kernels for 22%

commit v1 on v0

--- a/solution.py
+++ b/solution.py
@@ -11,99 +11,421 @@
 HIGHEST = lax.Precision.HIGHEST
 BLOCK = 128
 TILE = 8
-VMEM_LIMIT = 58 * 1024 * 1024
-
-
-def outer(left, right, precision=None):
-    return lax.dot_general(
-        left, right, (((0,), (0,)), ((), ())), precision=precision, preferred_element_type=jnp.float32
-    )
-
-
-def row_tile(rows):
-    for tile in (640, 512, 400, 320, 256, 160, 128, 64, 32, 16):
-        if rows % tile == 0:
-            return tile
-    return rows
-
-
-def sample_kernel(matrix, sketch, out):
-    out[...] = jnp.dot(matrix[...], sketch[...], preferred_element_type=jnp.float32).astype(out.dtype)
-
-
-def sample(matrix, sketch):
-    rows, depth = matrix.shape
-    width = sketch.shape[1]
-    tile = row_tile(rows)
+LANES = 128
+SLOTS = 3
+AHEAD = 2
+VMEM_LIMIT = 67043328
+
+
+def across(left, right):
+    return lax.dot_general(left, right, (((1,), (1,)), ((), ())), preferred_element_type=jnp.float32)
+
+
+def plan(part, n_row):
+    sub = LANES if part % LANES == 0 else part
+    pieces = part // sub
+    if pieces % 5 or pieces < 25:
+        return sub, pieces, 1, [pieces], pieces, [pieces - 1 + n_row], 0, 1
+    groups = []
+    while sum(groups) + 12 < pieces:
+        groups.append(6)
+    left = pieces - sum(groups)
+    groups += [left - left // 2 + left % 2, left // 2 - left % 2] if left > 6 else [left]
+    lead = sum(groups[:2])
+    lag, stride = 3, 8
+    total = pieces + lag + stride * (n_row - 1) - lead
+    parts = [5, 5]
+    total -= 10
+    for g in range(2, len(groups)):
+        parts.append(total // (len(groups) - g))
+        total -= parts[-1]
+    return sub, pieces, 5, groups, lead, parts, lag, stride
+
+
+def move_kernel(n_row, n_col, shape, corner, edge, sketch, corner_out, edge_out, cols, ring, images, mine, away, near, upper, lower, staged, rows, tmp, *sems):
+    (load_sem, near_send, near_recv, chain_send, upper_recv, lower_recv,
+     cast_send, cast_recv, back_send, back_recv, swap_send, swap_recv) = sems
+    sub, pieces, tiles, groups, lead, parts, lag, stride = shape
+    ratio = n_col // n_row
+    me_row, me_col = lax.axis_index("row"), lax.axis_index("col")
+    place, half = me_col // ratio, lax.rem(me_col, ratio)
+    part = cols.shape[1]
+    chunk = part // tiles
+    per_tile = pieces // tiles
+
+    owner = place == me_row
+    has_upper = jnp.logical_and(place >= me_row, place < n_row - 1)
+    has_lower = jnp.logical_and(place <= me_row, place > 0)
+    to_lower, to_upper = place > me_row, place < me_row
+    back_up = jnp.logical_and(place >= me_row, place < n_row - 1)
+    back_down = jnp.logical_and(place <= me_row, place > 0)
+
+    def partner(d):
+        return (me_row, place * ratio + lax.rem(half + d, ratio))
+
+    def peer(d):
+        return (lax.rem(me_row + d, n_row), me_col)
+
+    up_id = (me_row, lax.rem(me_col + ratio, n_col))
+    down_id = (me_row, lax.rem(me_col + n_col - ratio, n_col))
+
+    def remote(source, target, send, recv, device):
+        return pltpu.make_async_remote_copy(
+            src_ref=source, dst_ref=target, send_sem=send, recv_sem=recv,
+            device_id=device, device_id_type=pl.DeviceIdType.MESH,
+        )
+
+    def span(s, count=1):
+        if pieces == 1:
+            return pl.ds(0, sub)
+        return pl.ds(pl.multiple_of(s * sub, sub), count * sub)
+
+    def near_copy(d, s):
+        return remote(away.at[d - 1, :, span(s)], near.at[d - 1, :, span(s)],
+                      near_send.at[d - 1, s], near_recv.at[d - 1, s], partner(d))
+
+    def down_copy(s):
+        return remote(staged.at[:, span(s)], upper.at[:, span(s)], chain_send.at[s], upper_recv.at[s], down_id)
+
+    def up_copy(s):
+        return remote(staged.at[:, span(s)], lower.at[:, span(s)], chain_send.at[s], lower_recv.at[s], up_id)
+
+    def cast_copy(d, s):
+        return remote(rows.at[0, :, span(s)], cols.at[:, span(s)], cast_send.at[d - 1, s], cast_recv.at[s], peer(d))
+
+    def back_copy(way, s):
+        return remote(rows.at[0, :, span(s)], rows.at[0, :, span(s)], back_send.at[way, s], back_recv.at[s],
+                      up_id if way else down_id)
+
+    def swap_copy(d, s):
+        return remote(rows.at[0, :, span(s)], rows.at[ratio - d, :, span(s)],
+                      swap_send.at[d - 1, s], swap_recv.at[ratio - d - 1, s], partner(d))
+
+    starts = [sum(groups[:g]) for g in range(len(groups))]
+
+    def load(matrix, t, g, slot):
+        k0, width = starts[g] * sub, groups[g] * sub
+        copies = []
+        for pos in range(ratio):
+            at = pl.multiple_of(lax.rem(half + pos, ratio) * part + t * chunk, TILE * 2)
+            copies.append(pltpu.make_async_copy(
+                matrix.at[pl.ds(at, chunk), k0 : k0 + width], ring.at[slot, pos, :, 0:width], load_sem.at[slot, pos]))
+        return copies
+
+    def product(left, t, g, slot):
+        k0, width = starts[g] * sub, groups[g] * sub
+        operand = left[:, k0 : k0 + width]
+        if chunk % LANES == 0:
+            block = ring[slot, :, :, 0:width].reshape(ratio * chunk, width)
+            found = across(operand, block)
+            return [found[:, p * chunk : (p + 1) * chunk] for p in range(ratio)]
+        return [across(operand, ring[slot, p, :, 0:width]) for p in range(ratio)]
+
+    barrier = pltpu.get_barrier_semaphore()
+
+    def greet(device):
+        pl.semaphore_signal(barrier, inc=1, device_id=device, device_id_type=pl.DeviceIdType.MESH)
+
+    n_groups = len(groups)
+    steps = [("sample", g) for g in range(n_groups)]
+
+    def start_sample(t, g, slot):
+        for copy in load(corner, t, g, slot):
+            copy.start()
+
+    def start_image(m, t, g, slot):
+        for copy in load(edge if m else corner, t, g, slot):
+            copy.start()
+
+    total_sample = tiles * n_groups
+
+    def start_at(index):
+        if index < total_sample:
+            start_sample(index // n_groups, index % n_groups, index % SLOTS)
+        else:
+            index -= total_sample
+            g, rest = divmod(index, 2 * tiles)
+            start_image(rest % 2, rest // 2, g, (index + total_sample) % SLOTS)
+
+    for index in range(AHEAD):
+        start_at(index)
+    for d in range(1, ratio):
+        greet(partner(d))
+    for d in range(1, n_row):
+        greet(peer(d))
+
+    @pl.when(place < n_row - 1)
+    def _():
+        greet(up_id)
+
+    @pl.when(place > 0)
+    def _():
+        greet(down_id)
+
+    ends = (place < n_row - 1).astype(jnp.int32) + (place > 0).astype(jnp.int32)
+    pl.semaphore_wait(barrier, ratio - 1 + n_row - 1 + ends)
+
+    def gather(s):
+        total = mine[:, span(s)].astype(jnp.float32)
+        for d in range(1, ratio):
+            near_copy(d, s).wait_recv()
+            total += near[d - 1, :, span(s)].astype(jnp.float32)
+        tmp[...] = total
+
+        @pl.when(has_upper)
+        def _():
+            down_copy(s).wait_recv()
+            tmp[...] += upper[:, span(s)].astype(jnp.float32)
+
+        @pl.when(has_lower)
+        def _():
+            up_copy(s).wait_recv()
+            tmp[...] += lower[:, span(s)].astype(jnp.float32)
+
+        @pl.when(owner)
+        def _():
+            value = tmp[...].astype(jnp.bfloat16)
+            rows[0, :, span(s)] = value
+            cols[:, span(s)] = value
+            for d in range(1, n_row):
+                cast_copy(d, s).start()
+
+            @pl.when(place < n_row - 1)
+            def _():
+                back_copy(1, s).start()
+
+            @pl.when(place > 0)
+            def _():
+                back_copy(0, s).start()
+
+        @pl.when(to_lower)
+        def _():
+            staged[:, span(s)] = tmp[...].astype(jnp.bfloat16)
+            down_copy(s).start()
+
+        @pl.when(to_upper)
+        def _():
+            staged[:, span(s)] = tmp[...].astype(jnp.bfloat16)
+            up_copy(s).start()
+
+    def hand_back(s):
+        @pl.when(jnp.logical_not(owner))
+        def _():
+            back_copy(0, s).wait_recv()
+
+            @pl.when(jnp.logical_and(to_lower, place < n_row - 1))
+            def _():
+                back_copy(1, s).start()
+
+            @pl.when(jnp.logical_and(to_upper, place > 0))
+            def _():
+                back_copy(0, s).start()
+
+        for d in range(1, ratio):
+            swap_copy(d, s).start()
+
+    wait = lag + stride * jnp.abs(place - me_row)
+
+    def advance(first, p):
+        if first < pieces:
+            @pl.when(p < pieces)
+            def _():
+                gather(p)
+
+        @pl.when(jnp.logical_and(p >= wait, p < wait + pieces))
+        def _():
+            hand_back(p - wait)
+
+    def positions(first, count):
+        def one(i, carry):
+            advance(first, first + i)
+            return carry
+
+        lax.fori_loop(0, count, one, 0)
+
+    early = [0] * tiles
+    if tiles > 1:
+        early = [0, 0, 2, 2, 3]
+
+    def sample_tile(t, carry):
+        for g in range(n_groups):
+            index = t * n_groups + g
+            slot = lax.rem(index, SLOTS)
+            for copy in load(corner, t, g, slot):
+                copy.wait()
+            later = g + AHEAD
+            if later < n_groups:
+                start_sample(t, later, lax.rem(index + AHEAD, SLOTS))
+            else:
+                later_t, later_g = t + later // n_groups, later % n_groups
+
+                @pl.when(later_t < tiles)
+                def _():
+                    start_sample(later_t, later_g, lax.rem(index + AHEAD, SLOTS))
+
+            found = product(sketch, t, g, slot)
+            if g > 0:
+                found = [images[0, 0, p] + found[p] for p in range(ratio)]
+            if g < n_groups - 1:
+                for p in range(ratio):
+                    images[0, 0, p] = found[p]
+            else:
+                at = span(t * per_tile, per_tile)
+                mine[:, at] = found[0].astype(jnp.bfloat16)
+                for d in range(1, ratio):
+                    away[d - 1, :, at] = found[d].astype(jnp.bfloat16)
+        for d in range(1, ratio):
+            for i in range(per_tile):
+                near_copy(d, t * per_tile + i).start()
+        if tiles > 1:
+            before = jnp.where(t > 2, (t - 2) * 2, 0)
+            count = jnp.where(t < 2, 0, jnp.where(t == 4, 3, 2))
+
+            def one(i, inner):
+                advance(0, before + i)
+                return inner
+
+            lax.fori_loop(0, count, one, 0)
+        return carry
+
+    lax.fori_loop(0, tiles, sample_tile, 0)
+    done = sum(early)
+    for index in range(AHEAD):
+        start_at(total_sample + index)
+    positions(done, lead - done)
+
+    first = lead
+    for g in range(n_groups):
+        for i in range(groups[g]):
+            s = starts[g] + i
+
+            @pl.when(jnp.logical_not(owner))
+            def _():
+                cast_copy(1, s).wait_recv()
+
+        every = parts[g] // tiles
+
+        def image_tile(t, carry):
+            for m in range(2):
+                index = total_sample + (g * tiles + t) * 2 + m
+                slot = lax.rem(index, SLOTS)
+                for copy in load(edge if m else corner, t, g, slot):
+                    copy.wait()
+                ahead = t * 2 + m + AHEAD
+                into = lax.rem(index + AHEAD, SLOTS)
+
+                @pl.when(ahead < 2 * tiles)
+                def _():
+                    start_image(m, t + 1, g, into)
+
+                if g + 1 < n_groups:
+                    @pl.when(ahead >= 2 * tiles)
+                    def _():
+                        start_image(m, 0, g + 1, into)
+
+                found = product(cols, t, g, slot)
+                for p in range(ratio):
+                    if g == 0:
+                        images[m, t, p] = found[p]
+                    else:
+                        images[m, t, p] += found[p]
+            for i in range(every):
+                advance(first, first + t * every + i)
+            return carry
+
+        lax.fori_loop(0, tiles, image_tile, 0)
+        tail = parts[g] - every * tiles
+        if tail:
+            positions(first + every * tiles, tail)
+        first += parts[g]
+
+    corner_out[...] = jnp.zeros_like(corner_out)
+    edge_out[...] = jnp.zeros_like(edge_out)
+
+    def left_tile(t, carry):
+        for d in range(1, ratio):
+            for i in range(per_tile):
+                swap_copy(d, t * per_tile + i).wait_recv()
+        at = span(t * per_tile, per_tile)
+        for m, out in ((0, corner_out), (1, edge_out)):
+            if chunk % LANES == 0:
+                left = jnp.concatenate([rows[p, :, at] for p in range(ratio)], axis=1)
+                right = jnp.concatenate([images[m, t, p].astype(jnp.bfloat16) for p in range(ratio)], axis=1)
+                out[...] += across(left, right)
+            else:
+                for p in range(ratio):
+                    out[...] += across(rows[p, :, at], images[m, t, p].astype(jnp.bfloat16))
+        return carry
+
+    lax.fori_loop(0, tiles, left_tile, 0)
+
+    def finish(s, carry):
+        for d in range(1, ratio):
+            near_copy(d, s).wait_send()
+            swap_copy(d, s).wait_send()
+
+        @pl.when(owner)
+        def _():
+            for d in range(1, n_row):
+                cast_copy(d, s).wait_send()
+
+        @pl.when(jnp.logical_not(owner))
+        def _():
+            down_copy(s).wait_send()
+
+        @pl.when(back_up)
+        def _():
+            back_copy(1, s).wait_send()
+
+        @pl.when(back_down)
+        def _():
+            back_copy(0, s).wait_send()
+
+        return carry
+
+    lax.fori_loop(0, pieces, finish, 0)
+
+
+def move(corner, edge, sketch):
+    n_row, n_col = lax.axis_size("row"), lax.axis_size("col")
+    height, part = corner.shape
+    width = sketch.shape[0]
+    ratio = n_col // n_row
+    assert ratio * n_row == n_col and height == ratio * part
+    shape = plan(part, n_row)
+    sub, pieces, tiles, groups = shape[:4]
+    chunk = part // tiles
+    dma = pltpu.SemaphoreType.DMA
+    half = jnp.bfloat16
+    square = jax.ShapeDtypeStruct((width, width), jnp.float32)
+    vmem = pl.BlockSpec(memory_space=pltpu.VMEM)
+    hbm = pl.BlockSpec(memory_space=pl.ANY)
     return pl.pallas_call(
-        sample_kernel,
-        grid=(rows // tile,),
-        out_shape=jax.ShapeDtypeStruct((rows, width), jnp.bfloat16),
-        in_specs=[
-            pl.BlockSpec((tile, depth), lambda i: (i, 0)),
-            pl.BlockSpec((depth, width), lambda i: (0, 0)),
+        functools.partial(move_kernel, n_row, n_col, shape),
+        out_shape=(square, square, jax.ShapeDtypeStruct((width, part), half)),
+        in_specs=[hbm, hbm, vmem],
+        out_specs=(vmem, vmem, vmem),
+        scratch_shapes=[
+            pltpu.VMEM((SLOTS, ratio, chunk, max(groups) * sub), half),
+            pltpu.VMEM((2, tiles, ratio, width, chunk), jnp.float32),
+            pltpu.VMEM((width, part), half),
+            pltpu.VMEM((ratio - 1, width, part), half),
+            pltpu.VMEM((ratio - 1, width, part), half),
+            pltpu.VMEM((width, part), half),
+            pltpu.VMEM((width, part), half),
+            pltpu.VMEM((width, part), half),
+            pltpu.VMEM((ratio, width, part), half),
+            pltpu.VMEM((width, sub), jnp.float32),
+            dma((SLOTS, ratio)),
+            dma((ratio - 1, pieces)), dma((ratio - 1, pieces)),
+            dma((pieces,)), dma((pieces,)), dma((pieces,)),
+            dma((n_row - 1, pieces)), dma((pieces,)),
+            dma((2, pieces)), dma((pieces,)),
+            dma((ratio - 1, pieces)), dma((ratio - 1, pieces)),
         ],
-        out_specs=pl.BlockSpec((tile, width), lambda i: (i, 0)),
-        compiler_params=pltpu.CompilerParams(vmem_limit_bytes=VMEM_LIMIT),
-    )(matrix, sketch)
-
-
-def image_kernel(matrix, cols, out):
-    out[...] = jnp.dot(matrix[...], cols[...], preferred_element_type=jnp.float32)
-
-
-def image_of(matrix, cols):
-    height, depth = matrix.shape
-    width = cols.shape[1]
-    tile = row_tile(height)
-    return pl.pallas_call(
-        image_kernel,
-        grid=(height // tile,),
-        out_shape=jax.ShapeDtypeStruct((height, width), jnp.float32),
-        in_specs=[
-            pl.BlockSpec((tile, depth), lambda i: (i, 0)),
-            pl.BlockSpec((depth, width), lambda i: (0, 0)),
-        ],
-        out_specs=pl.BlockSpec((tile, width), lambda i: (i, 0)),
-        cost_estimate=pl.CostEstimate(
-            flops=2 * height * depth * width, bytes_accessed=2 * height * depth, transcendentals=0
-        ),
-        compiler_params=pltpu.CompilerParams(vmem_limit_bytes=VMEM_LIMIT),
-    )(matrix, cols)
-
-
-def left_kernel(rows, first, second, first_out, second_out):
-    left = rows[...].T
-
-    def term(image):
-        upper_part = image.astype(jnp.bfloat16)
-        lower_part = (image - upper_part.astype(jnp.float32)).astype(jnp.bfloat16)
-        found = jnp.dot(left, upper_part, preferred_element_type=jnp.float32)
-        return found + jnp.dot(left, lower_part, preferred_element_type=jnp.float32)
-
-    @pl.when(pl.program_id(0) == 0)
-    def _():
-        first_out[...] = jnp.zeros_like(first_out)
-        second_out[...] = jnp.zeros_like(second_out)
-
-    first_out[...] += term(first[...])
-    second_out[...] += term(second[...])
-
-
-def left_products(rows, first, second):
-    height, width = rows.shape
-    tile = row_tile(height)
-    tall = pl.BlockSpec((tile, width), lambda i: (i, 0))
-    square = pl.BlockSpec((width, width), lambda i: (0, 0))
-    shape = jax.ShapeDtypeStruct((width, width), jnp.float32)
-    return pl.pallas_call(
-        left_kernel,
-        grid=(height // tile,),
-        out_shape=(shape, shape),
-        in_specs=[tall, tall, tall],
-        out_specs=(square, square),
-        compiler_params=pltpu.CompilerParams(vmem_limit_bytes=VMEM_LIMIT),
-    )(rows, first, second)
+        compiler_params=pltpu.CompilerParams(
+            collective_id=2, has_side_effects=True, vmem_limit_bytes=VMEM_LIMIT),
+    )(corner, edge, sketch)
 
 
 def eliminate(block):
@@ -279,33 +601,16 @@
     return result[:height]
 
 
-def column_route(n_row, n_col):
-    ratio = n_col // n_row
-    route = []
-    for source in range(n_row):
-        for shard in range(n_col):
-            half, target = divmod(shard, n_row)
-            route.append((source * n_col + shard, target * n_col + source * ratio + half))
-    return route
-
-
 def body(corner, edge, sketch):
-    n_row, n_col = lax.axis_size("row"), lax.axis_size("col")
-    both = ("row", "col")
-    shard = lax.psum_scatter(sample(corner, sketch), "col", scatter_dimension=0, tiled=True)
-    gram = reduce_all(outer(shard, shard), 0)
-    shard, gram = lax.optimization_barrier((shard, gram))
-    moved = lax.ppermute(shard, both, column_route(n_row, n_col))
-    cols = lax.all_gather(moved, "row", axis=0, tiled=True)
-    rows = lax.all_gather(shard, "col", axis=0, tiled=True)
+    n_row = lax.axis_size("row")
+    corner_sum, edge_sum, cols = move(corner, edge, sketch.T)
+    gram = reduce_all(across(cols, cols) * (1.0 / n_row), 0)
     inverse = inverse_factor(gram)
-    corner_image, edge_image = image_of(corner, cols), image_of(edge, cols)
 
     def renormalize(total):
         half = jnp.dot(inverse, total, precision=HIGHEST)
         return lax.dot_general(half, inverse, (((1,), (1,)), ((), ())), precision=HIGHEST)
 
-    corner_sum, edge_sum = left_products(rows, corner_image, edge_image)
     stacked = jnp.concatenate([renormalize(corner_sum), renormalize(edge_sum)], axis=0)
     result = reduce_all(stacked, 1)
     return result[:RANK], result[RANK:]

time: 497 us -> 338 us (0.68)
  waiting for transfers between devices: 169 us -> 0 us
  Pallas kernels: 269 us -> 318 us
  local copies, waits for them, and re-layouts: 31.2 us -> 6.01 us
  between operations: 13.9 us -> 0.71 us
    reduce_scatter x1 -> x0, waiting for transfers between devices: 121 us -> none  [body(): lax.psum_scatter(sample(corner, sketch), 'col', scatter_dimension=0, tile...]
    all_gather x2 -> x0, waiting for transfers between devices: 47.9 us -> none  [the longest x1 35.8 us: body(): rows = lax.all_gather(shard, 'col', axis=0, tiled=True)]
    pallas_call x4 -> x1, Pallas kernels: 109 us -> 148 us  [move(): pl.pallas_call(functools.partial(move_kernel, n_row, n_col, shape), out_s...]
    all_gather x2 -> x0, local copies, waits for them, and re-layouts: 16.8 us -> none  [the longest x1 11 us: body(): rows = lax.all_gather(shard, 'col', axis=0, tiled=True)]
    pallas_call x2, Pallas kernels: 108 us -> 118 us  [reduce_all(): pl.pallas_call(functools.partial(reduce_kernel, n_row, n_col), out_shape=...]
    unnamed x10 -> x6, local copies, waits for them, and re-layouts: 7.57 us -> 0.01 us
  transfers between devices with their start and end apart: 4 -> 0, of which waited for: 3 -> 0; matrix products, arithmetic and copies ran while one was open for 1% -> 0% of each run, Pallas kernels for 22% -> 0%
where the time goes in v1:
time: 338 us; the launch traced here: 337 us
  Pallas kernels  318 us (94%)
  matrix products  11.6 us (3%)
  local copies, waits for them, and re-layouts  6.01 us (2%)
    pallas_call x1, Pallas kernels, move(): pl.pallas_call(functools.partial(move_kernel, n_row, n_col, shape), out_s...  148 us
    pallas_call x2, Pallas kernels, reduce_all(): pl.pallas_call(functools.partial(reduce_kernel, n_row, n_col), out_shape=...  118 us
    pallas_call x1, Pallas kernels, inverse_factor(): pl.pallas_call(factor_kernel, out_shape=jax.ShapeDtypeStruct((size, size)...  51.7 us

profile of v1, /device:TPU:31, one launch (start us, length us, event | category | flops | bytes accessed | tf_op | source)
XLA Modules:
  0.0 337.4 jit_solution(1263928126525333679)
XLA Ops:
  0.6 148.0 %shard_map.50 = (f32[448,448]{1,0:T(8,128)}, f32[448,448]{1,0:T(8,128)}, bf16[448,3200]{1,0:T(8,128)(2,1)}) custom-call(bf16[6400,3200]{1,0:T(8,128)(2,1)} %corner.1, bf16[6400,3200]{1,0:T(8,128)(2,1)} %edge.1, bf16[448,3200]{1,0:T(8,128)(2,1)} %bitcast.7), custom_call_target="tpu_custom_call" | custom-call | tf_op jit(solution)/shard_map/pallas_call | solution.py:403
  148.6 4.4 %convolution_multiply_fusion = f32[448,448]{1,0:T(8,128)S(1)} fusion(bf16[448,3200]{1,0:T(8,128)(2,1)} %get-tuple-element.5), kind=kOutput, calls=%fused_computation.2 | convolution fusion | flops 1284706304 | bytes 3670016 | tf_op jit(solution)/shard_map/dot_general | solution.py:21
  153.0 1.1 pad.8.x
  154.1 53.5 %shard_map.51 = f32[512,448]{1,0:T(8,128)} custom-call(f32[512,448]{1,0:T(8,128)} %pad.8.x), custom_call_target="tpu_custom_call" | custom-call | tf_op jit(solution)/shard_map/pallas_call | solution.py:586
  207.6 2.2 slice.15.gram
  209.8 0.0 copy-start.2
  209.8 51.7 %shard_map.52 = f32[448,448]{1,0:T(8,128)} custom-call(f32[448,448]{1,0:T(8,128)} %slice.15.gram), custom_call_target="tpu_custom_call" | custom-call | flops 13421772800 | bytes 1605632 | tf_op jit(solution)/shard_map/pallas_call | solution.py:491
  261.5 0.0 copy-done.2
  261.5 0.0 copy-start
  261.5 0.0 copy-start.1
  261.5 2.8 fusion.2
  264.3 0.0 copy-done
  264.3 0.0 copy-done.1
  264.3 1.5 fusion.6
  265.8 1.5 fusion.4
  267.3 1.5 fusion
  268.8 1.6 select_maximum_fusion.x
  270.4 64.4 %shard_map.53 = f32[1024,400]{1,0:T(8,128)} custom-call(f32[1024,400]{1,0:T(8,128)} %select_maximum_fusion.x), custom_call_target="tpu_custom_call" | custom-call | tf_op jit(solution)/shard_map/pallas_call | solution.py:586
  334.7 2.7 fusion.8
Async XLA Ops:
  209.8 51.7 %copy-start.2 = (f32[448,448]{1,0:T(8,128)S(1)}, f32[448,448]{1,0:T(8,128)}, u32[]{:S(2)}) copy-start(f32[448,448]{1,0:T(8,128)} %get-tuple-element.7) | copy-start | bytes 2408452
  261.5 2.8 copy-start
  261.5 2.8 copy-start.1

commit v2 on v1

v2 whole, which is shorter than its diff:
```python
import functools

import jax
import jax.numpy as jnp
from jax import lax
from jax.experimental import pallas as pl
from jax.experimental.pallas import tpu as pltpu
from jax.sharding import PartitionSpec as P

RANK = 400
HIGHEST = lax.Precision.HIGHEST
BLOCK = 128
TILE = 8
LANES = 128
SLOTS = 3
AHEAD = 2
VMEM_LIMIT = 67043328


def across(left, right):
    return lax.dot_general(left, right, (((1,), (1,)), ((), ())), preferred_element_type=jnp.float32)


def plan(part, n_row):
    sub = LANES if part % LANES == 0 else part
    pieces = part // sub
    if pieces % 5 or pieces < 25:
        return sub, pieces, 1, [pieces], pieces, [pieces - 1 + n_row], 0, 1, 0
    groups = []
    while sum(groups) + 12 < pieces:
        groups.append(6)
    left = pieces - sum(groups)
    groups += [left - left // 2 + left % 2, left // 2 - left % 2] if left > 6 else [left]
    lead = sum(groups[:2])
    lag, stride = 3, 5
    total = pieces + lag + stride * (n_row - 1) - lead
    parts = [6, 6]
    total -= 12
    for g in range(2, len(groups)):
        parts.append(total // (len(groups) - g))
        total -= parts[-1]
    return sub, pieces, 5, groups, lead, parts, lag, stride, pieces - 3


def move_kernel(n_row, n_col, shape, corner, edge, sketch, sums, gram, cols, ring, images, mine, away, near, upper, lower, rows, scratch, square, land, piece, *sems):
    (load_sem, near_send, near_recv, chain_send, upper_recv, lower_recv,
     cast_send, cast_recv, back_send, back_recv, swap_send, swap_recv,
     fold_send, fold_recv, part_send, part_recv, full_send, full_recv) = sems
    sub, pieces, tiles, groups, lead, parts, lag, stride, hold = shape
    ratio = n_col // n_row
    me_row, me_col = lax.axis_index("row"), lax.axis_index("col")
    place, half = me_col // ratio, lax.rem(me_col, ratio)
    part = cols.shape[1]
    chunk = part // tiles
    tmp = scratch if pieces > 1 else images.at[0, 0, 0]
    per_tile = pieces // tiles

    owner = place == me_row
    has_upper = jnp.logical_and(place >= me_row, place < n_row - 1)
    has_lower = jnp.logical_and(place <= me_row, place > 0)
    to_lower, to_upper = place > me_row, place < me_row
    back_up = jnp.logical_and(place >= me_row, place < n_row - 1)
    back_down = jnp.logical_and(place <= me_row, place > 0)

    def partner(d):
        return (me_row, place * ratio + lax.rem(half + d, ratio))

    def peer(d):
        return (lax.rem(me_row + d, n_row), me_col)

    def column(d):
        return (me_row, lax.rem(me_col + d, n_col))

    up_id = (me_row, lax.rem(me_col + ratio, n_col))
    down_id = (me_row, lax.rem(me_col + n_col - ratio, n_col))

    def remote(source, target, send, recv, device):
        return pltpu.make_async_remote_copy(
            src_ref=source, dst_ref=target, send_sem=send, recv_sem=recv,
            device_id=device, device_id_type=pl.DeviceIdType.MESH,
        )

    def span(s, count=1):
        if pieces == 1:
            return pl.ds(0, sub)
        return pl.ds(pl.multiple_of(s * sub, sub), count * sub)

    def near_copy(d, s):
        return remote(away.at[d - 1, :, span(s)], near.at[d - 1, :, span(s)],
                      near_send.at[d - 1, s], near_recv.at[d - 1, s], partner(d))

    def down_copy(s):
        return remote(mine.at[:, span(s)], upper.at[:, span(s)], chain_send.at[s], upper_recv.at[s], down_id)

    def up_copy(s):
        return remote(mine.at[:, span(s)], lower.at[:, span(s)], chain_send.at[s], lower_recv.at[s], up_id)

    def cast_copy(d, s):
        return remote(rows.at[0, :, span(s)], cols.at[:, span(s)], cast_send.at[d - 1, s], cast_recv.at[s], peer(d))

    def back_copy(way, s):
        return remote(rows.at[0, :, span(s)], rows.at[0, :, span(s)], back_send.at[way, s], back_recv.at[s],
                      up_id if way else down_id)

    def swap_copy(d, s):
        return remote(rows.at[0, :, span(s)], rows.at[ratio - d, :, span(s)],
                      swap_send.at[d - 1, s], swap_recv.at[ratio - d - 1, s], partner(d))

    starts = [sum(groups[:g]) for g in range(len(groups))]

    def load(matrix, t, g, slot):
        k0, width = starts[g] * sub, groups[g] * sub
        copies = []
        for pos in range(ratio):
            at = pl.multiple_of(lax.rem(half + pos, ratio) * part + t * chunk, TILE * 2)
            copies.append(pltpu.make_async_copy(
                matrix.at[pl.ds(at, chunk), k0 : k0 + width], ring.at[slot, pos, :, 0:width], load_sem.at[slot, pos]))
        return copies

    def product(left, t, g, slot):
        k0, width = starts[g] * sub, groups[g] * sub
        operand = left[:, k0 : k0 + width]
        if chunk % LANES == 0:
            block = ring[slot, :, :, 0:width].reshape(ratio * chunk, width)
            found = across(operand, block)
            return [found[:, p * chunk : (p + 1) * chunk] for p in range(ratio)]
        return [across(operand, ring[slot, p, :, 0:width]) for p in range(ratio)]

    barrier = pltpu.get_barrier_semaphore()

    def greet(device):
        pl.semaphore_signal(barrier, inc=1, device_id=device, device_id_type=pl.DeviceIdType.MESH)

    n_groups = len(groups)
    steps = [("sample", g) for g in range(n_groups)]

    def start_sample(t, g, slot):
        for copy in load(corner, t, g, slot):
            copy.start()

    def start_image(m, t, g, slot):
        for copy in load(edge if m else corner, t, g, slot):
            copy.start()

    total_sample = tiles * n_groups

    def start_at(index):
        if index < total_sample:
            start_sample(index // n_groups, index % n_groups, index % SLOTS)
        else:
            index -= total_sample
            g, rest = divmod(index, 2 * tiles)
            start_image(rest % 2, rest // 2, g, (index + total_sample) % SLOTS)

    for index in range(AHEAD):
        start_at(index)
    for d in range(1, n_row):
        greet(peer(d))
    for d in range(1, n_col):
        greet(column(d))
    pl.semaphore_wait(barrier, n_row + n_col - 2)

    def gather(s):
        total = mine[:, span(s)].astype(jnp.float32)
        for d in range(1, ratio):
            near_copy(d, s).wait_recv()
            total += near[d - 1, :, span(s)].astype(jnp.float32)
        tmp[...] = total

        @pl.when(has_upper)
        def _():
            down_copy(s).wait_recv()
            tmp[...] += upper[:, span(s)].astype(jnp.float32)

        @pl.when(has_lower)
        def _():
            up_copy(s).wait_recv()
            tmp[...] += lower[:, span(s)].astype(jnp.float32)

        @pl.when(owner)
        def _():
            value = tmp[...].astype(jnp.bfloat16)
            rows[0, :, span(s)] = value
            cols[:, span(s)] = value
            for d in range(1, n_row):
                cast_copy(d, s).start()

            @pl.when(place < n_row - 1)
            def _():
                back_copy(1, s).start()

            @pl.when(place > 0)
            def _():
                back_copy(0, s).start()

        @pl.when(to_lower)
        def _():
            mine[:, span(s)] = tmp[...].astype(jnp.bfloat16)
            down_copy(s).start()

        @pl.when(to_upper)
        def _():
            mine[:, span(s)] = tmp[...].astype(jnp.bfloat16)
            up_copy(s).start()

    prompt = pieces - 10 if pieces > 10 else pieces

    def hand_back(s):
        @pl.when(jnp.logical_not(owner))
        def _():
            back_copy(0, s).wait_recv()

            @pl.when(jnp.logical_and(to_lower, place < n_row - 1))
            def _():
                back_copy(1, s).start()

            @pl.when(jnp.logical_and(to_upper, place > 0))
            def _():
                back_copy(0, s).start()

    def swap(first, last):
        for s in range(first, last):
            for d in range(1, ratio):
                swap_copy(d, s).start()

    wait = lag + stride * jnp.abs(place - me_row)

    def advance(first, p):
        if first < pieces:
            @pl.when(p < pieces)
            def _():
                gather(p)

        @pl.when(jnp.logical_and(p >= wait, p < wait + pieces))
        def _():
            hand_back(p - wait)

        turn = p - jnp.maximum(wait, hold)

        @pl.when(jnp.logical_and(turn >= 0, turn < prompt))
        def _():
            for d in range(1, ratio):
                swap_copy(d, turn).start()

    def positions(first, start, stop):
        def one(p, carry):
            advance(first, p)
            return carry

        lax.fori_loop(start, stop, one, 0)

    source = jnp.where(to_lower, n_row - 1 - place, jnp.where(to_upper, place, jnp.maximum(n_row - 1 - place, place)))

    def early(t):
        return jnp.clip(2 * t - 1 - 2 * source, 0, lead) if tiles > 1 else 0

    begin = jnp.maximum(groups[0], lead - 2 * source)
    floor = max(groups[0], lead - 2 * (n_row - 1))

    def sample_tile(t, carry):
        for g in range(n_groups):
            index = t * n_groups + g
            slot = lax.rem(index, SLOTS)
            for copy in load(corner, t, g, slot):
                copy.wait()
            later = g + AHEAD
            if later < n_groups:
                start_sample(t, later, lax.rem(index + AHEAD, SLOTS))
            else:
                later_t, later_g = t + later // n_groups, later % n_groups

                @pl.when(later_t < tiles)
                def _():
                    start_sample(later_t, later_g, lax.rem(index + AHEAD, SLOTS))

            found = product(sketch, t, g, slot)
            if g > 0:
                found = [images[0, 0, p] + found[p] for p in range(ratio)]
            if g < n_groups - 1:
                for p in range(ratio):
                    images[0, 0, p] = found[p]
            else:
                at = span(t * per_tile, per_tile)
                mine[:, at] = found[0].astype(jnp.bfloat16)
                for d in range(1, ratio):
                    away[d - 1, :, at] = found[d].astype(jnp.bfloat16)
        for d in range(1, ratio):
            for i in range(per_tile):
                near_copy(d, t * per_tile + i).start()
        if tiles > 1:
            positions(0, early(t - 1), early(t))
        return carry

    lax.fori_loop(0, tiles, sample_tile, 0)
    for index in range(AHEAD):
        start_at(total_sample + index)
    positions(0, early(tiles - 1), begin)

    first = 0
    for g in range(n_groups):
        for i in range(groups[g]):
            s = starts[g] + i

            @pl.when(jnp.logical_not(owner))
            def _():
                cast_copy(1, s).wait_recv()

        every = parts[g] // tiles

        def image_tile(t, carry):
            for m in range(2):
                index = total_sample + (g * tiles + t) * 2 + m
                slot = lax.rem(index, SLOTS)
                for copy in load(edge if m else corner, t, g, slot):
                    copy.wait()
                ahead = t * 2 + m + AHEAD
                into = lax.rem(index + AHEAD, SLOTS)

                @pl.when(ahead < 2 * tiles)
                def _():
                    start_image(m, t + 1, g, into)

                if g + 1 < n_groups:
                    @pl.when(ahead >= 2 * tiles)
                    def _():
                        start_image(m, 0, g + 1, into)

                found = product(cols, t, g, slot)
                for p in range(ratio):
                    if g == 0:
                        images[m, t, p] = found[p]
                    else:
                        images[m, t, p] += found[p]
            for i in range(every):
                advance(floor + first, begin + first + t * every + i)
            return carry

        lax.fori_loop(0, tiles, image_tile, 0)
        tail = parts[g] - every * tiles
        if tail:
            positions(floor + first, begin + first + every * tiles, begin + first + parts[g])
        first += parts[g]

    width, padded = cols.shape[0], square.shape[0]
    big = padded // n_row
    small = big // n_col

    def at_rows(index, size):
        return pl.ds(pl.multiple_of(index, TILE), size)

    square[0:width, :] = across(cols[...], cols[...])
    if padded > width:
        square[width:padded, :] = jnp.zeros((padded - width, width), jnp.float32)
    folds, pieces_out, fulls = [], [], []
    for d in range(1, n_col):
        chunk_at = me_row * big + lax.rem(me_col + d, n_col) * small
        folds.append(remote(square.at[at_rows(chunk_at, small), :], land.at[d - 1],
                            fold_send.at[d - 1], fold_recv.at[d - 1], column(d)))
        folds[-1].start()
    swap(prompt, min(prompt + 3, pieces))
    own = at_rows(me_row * big + me_col * small, small)
    summed = square[own, :]
    for d in range(1, n_col):
        folds[d - 1].wait_recv()
        summed += land[d - 1]
    piece[...] = summed
    for d in range(1, n_col):
        pieces_out.append(remote(piece, gram.at[own, :], part_send.at[d - 1], part_recv.at[d - 1], column(d)))
        pieces_out[-1].start()
    swap(min(prompt + 3, pieces), pieces)
    gram[own, :] = summed
    for d in range(1, n_col):
        pieces_out[d - 1].wait_recv()
    block = gram.at[at_rows(me_row * big, big), :]
    for d in range(1, n_row):
        fulls.append(remote(block, block, full_send.at[d - 1], full_recv.at[d - 1], peer(d)))
        fulls[-1].start()

    sums[...] = jnp.zeros_like(sums)

    def left_tile(t, carry):
        for d in range(1, ratio):
            for i in range(per_tile):
                swap_copy(d, t * per_tile + i).wait_recv()
        at = span(t * per_tile, per_tile)

        def both(p):
            return jnp.concatenate([images[m, t, p] for m in range(2)], axis=0).astype(jnp.bfloat16)

        if chunk % LANES == 0:
            left = jnp.concatenate([rows[p, :, at] for p in range(ratio)], axis=1)
            right = jnp.concatenate([both(p) for p in range(ratio)], axis=1)
            sums[...] += across(left, right)
        else:
            for p in range(ratio):
                sums[...] += across(rows[p, :, at], both(p))
        return carry

    lax.fori_loop(0, tiles, left_tile, 0)
    for sent in fulls:
        sent.wait_recv()
    for sent in folds + pieces_out + fulls:
        sent.wait_send()

    def finish(s, carry):
        for d in range(1, ratio):
            near_copy(d, s).wait_send()
            swap_copy(d, s).wait_send()

        @pl.when(owner)
        def _():
            for d in range(1, n_row):
                cast_copy(d, s).wait_send()

        @pl.when(jnp.logical_not(owner))
        def _():
            down_copy(s).wait_send()

        @pl.when(back_up)
        def _():
            back_copy(1, s).wait_send()

        @pl.when(back_down)
        def _():
            back_copy(0, s).wait_send()

        return carry

    lax.fori_loop(0, pieces, finish, 0)


def move(corner, edge, sketch):
    n_row, n_col = lax.axis_size("row"), lax.axis_size("col")
    height, part = corner.shape
    width = sketch.shape[0]
    ratio = n_col // n_row
    assert ratio * n_row == n_col and height == ratio * part
    shape = plan(part, n_row)
    sub, pieces, tiles, groups = shape[:4]
    chunk = part // tiles
    dma = pltpu.SemaphoreType.DMA
    half = jnp.bfloat16
    grain = n_row * n_col * TILE
    padded = -(-width // grain) * grain
    small = padded // (n_row * n_col)
    vmem = pl.BlockSpec(memory_space=pltpu.VMEM)
    hbm = pl.BlockSpec(memory_space=pl.ANY)
    return pl.pallas_call(
        functools.partial(move_kernel, n_row, n_col, shape),
        out_shape=(jax.ShapeDtypeStruct((width, 2 * width), jnp.float32),
                   jax.ShapeDtypeStruct((padded, width), jnp.float32)),
        in_specs=[hbm, hbm, vmem],
        out_specs=(vmem, vmem),
        scratch_shapes=[
            pltpu.VMEM((width, part), half),
            pltpu.VMEM((SLOTS, ratio, chunk, max(groups) * sub), half),
            pltpu.VMEM((2, tiles, ratio, width, chunk), jnp.float32),
            pltpu.VMEM((width, part), half),
            pltpu.VMEM((ratio - 1, width, part), half),
            pltpu.VMEM((ratio - 1, width, part), half),
            pltpu.VMEM((width, part), half),
            pltpu.VMEM((width, part), half),
            pltpu.VMEM((ratio, width, part), half),
            pltpu.VMEM((width, sub) if pieces > 1 else (TILE, LANES), jnp.float32),
            pltpu.VMEM((padded, width), jnp.float32),
            pltpu.VMEM((n_col - 1, small, width), jnp.float32),
            pltpu.VMEM((small, width), jnp.float32),
            dma((SLOTS, ratio)),
            dma((ratio - 1, pieces)), dma((ratio - 1, pieces)),
            dma((pieces,)), dma((pieces,)), dma((pieces,)),
            dma((n_row - 1, pieces)), dma((pieces,)),
            dma((2, pieces)), dma((pieces,)),
            dma((ratio - 1, pieces)), dma((ratio - 1, pieces)),
            dma((n_col - 1,)), dma((n_col - 1,)), dma((n_col - 1,)), dma((n_col - 1,)),
            dma((n_row - 1,)), dma((n_row - 1,)),
        ],
        compiler_params=pltpu.CompilerParams(
            collective_id=2, has_side_effects=True, vmem_limit_bytes=VMEM_LIMIT),
    )(corner, edge, sketch)


def eliminate(block):
    size = block.shape[0]
    count = size // TILE
    lane = lax.broadcasted_iota(jnp.int32, (TILE, BLOCK), 1)
    line = lax.broadcasted_iota(jnp.int32, (2 * TILE, BLOCK), 0)
    work = [block[t * TILE : (t + 1) * TILE, :] for t in range(count)]
    top = lax.broadcasted_iota(jnp.int32, (TILE, BLOCK), 0)
    other = [(lane == top + t * TILE).astype(jnp.float32) for t in range(count)]
    done = []
    for h in range(count):
        at = h * TILE
        tiles = [h, h + 1] if h + 1 < count else [h]
        high = len(tiles) * TILE
        pair = jnp.concatenate([work[t] for t in tiles], axis=0)
        held = jnp.concatenate([other[t] for t in tiles], axis=0)
        fixed = [jnp.broadcast_to(pair[:, at + k : at + k + 1], (high, BLOCK)) for k in range(TILE)]
        ids = line[:high]
        for k in range(TILE):
            scale = 1.0 / fixed[k][k : k + 1, :]
            factor = jnp.where(ids > k, fixed[k] * scale, 0.0)
            pair = pair - factor * pair[k : k + 1, :]
            held = held - factor * held[k : k + 1, :]
            for j in range(k + 1, TILE):
                fixed[j] = fixed[j] - factor * fixed[j][k : k + 1, :]
        pivot = fixed[0][:TILE]
        for k in range(1, TILE):
            pivot = jnp.where(top == k, fixed[k][:TILE], pivot)
        upper, extra = pair[:TILE], held[:TILE]
        done.append(extra / jnp.sqrt(pivot))
        if h + 1 < count:
            work[h + 1], other[h + 1] = pair[TILE:], held[TILE:]
        if h + 2 < count:
            low = (h + 2) * TILE
            both = jnp.concatenate([upper / pivot, extra / pivot], axis=1)
            update = lax.dot_general(
                jnp.where(lane >= low, upper, 0.0), both, (((0,), (0,)), ((), ())),
                precision=HIGHEST, preferred_element_type=jnp.float32)
            for t in range(h + 2, count):
                work[t] = work[t] - update[t * TILE : (t + 1) * TILE, :BLOCK]
                other[t] = other[t] - update[t * TILE : (t + 1) * TILE, BLOCK:]
    return jnp.concatenate(done, axis=0)


def finish_kernel(n_row, n_col, sums, gram, total, inverse_out, x, out, held, *rest):
    lands, sems = rest[:3], rest[3:]
    me_row, me_col = lax.axis_index("row"), lax.axis_index("col")
    inner, outer = lax.rem(me_row, 2), me_row // 2
    counts = [2, n_row // 2, n_col]
    mine = [inner, outer, me_col]

    def device(level, d):
        other = lax.rem(mine[level] + d, counts[level])
        return [(outer * 2 + other, me_col), (other * 2 + inner, me_col), (me_row, other)][level]

    def copy(source, target, send, recv, where):
        return pltpu.make_async_remote_copy(
            src_ref=source, dst_ref=target, send_sem=send, recv_sem=recv,
            device_id=where, device_id_type=pl.DeviceIdType.MESH,
        )

    barrier = pltpu.get_barrier_semaphore()
    for level in range(3):
        for d in range(1, counts[level]):
            pl.semaphore_signal(barrier, inc=1, device_id=device(level, d), device_id_type=pl.DeviceIdType.MESH)

    size = gram.shape[1]
    tall, wide = size // TILE, 2 * size // LANES
    for j in range(wide):
        x[j * tall : (j + 1) * tall] = sums[:, j * LANES : (j + 1) * LANES].reshape(tall, TILE, LANES)
    if x.shape[0] > tall * wide:
        x[tall * wide :] = jnp.zeros((x.shape[0] - tall * wide, TILE, LANES), jnp.float32)
    padded = held.shape[0]
    ids_r = lax.broadcasted_iota(jnp.int32, (padded, padded), 0)
    ids_c = lax.broadcasted_iota(jnp.int32, (padded, padded), 1)
    unit = (ids_r == ids_c).astype(jnp.float32)
    held[:, :padded] = unit
    held[:, padded:] = unit
    held[:size, :size] = gram[:size, :]

    bases, sizes = [0], []
    for level in range(3):
        sizes.append((sizes[-1] if sizes else x.shape[0]) // counts[level])
        bases.append(bases[-1] + mine[level] * sizes[-1])

    def scatter(level):
        m = sizes[level]
        return [copy(x.at[pl.ds(bases[level] + lax.rem(mine[level] + d, counts[level]) * m, m)],
                     lands[level].at[d - 1], sems[4 * level].at[d - 1], sems[4 * level + 1].at[d - 1], device(level, d))
                for d in range(1, counts[level])]

    def spread(level):
        block = out.at[pl.ds(bases[level + 1], sizes[level])]
        return [copy(block, block, sems[4 * level + 2].at[d - 1], sems[4 * level + 3].at[d - 1], device(level, d))
                for d in range(1, counts[level])]

    def fold(level):
        own = pl.ds(bases[level + 1], sizes[level])
        value = x[own]
        for d, sent in enumerate(scatter(level)):
            sent.wait_recv()
            value += lands[level][d]
        if level == 2:
            out[own] = value
        else:
            x[own] = value

    def begin(copies):
        for sent in copies:
            sent.start()

    def arrive(copies):
        for sent in copies:
            sent.wait_recv()

    pl.semaphore_wait(barrier, sum(counts) - 3)
    begin(scatter(0))
    fold(0)
    begin(scatter(1))

    def stage(i):
        if i == 0:
            fold(1)
            begin(scatter(2))
        elif i == 1:
            fold(2)
            begin(spread(2))
        elif i == 2:
            arrive(spread(2))
            begin(spread(1))
        else:
            arrive(spread(1))
            begin(spread(0))

    blocks = padded // BLOCK

    def one(k, carry):
        at = pl.multiple_of(k * BLOCK, BLOCK)
        inverse = eliminate(held[pl.ds(at, BLOCK), pl.ds(at, BLOCK)])
        strip = jnp.dot(inverse, held[pl.ds(at, BLOCK), :], precision=HIGHEST, preferred_element_type=jnp.float32)
        held[pl.ds(at, BLOCK), :] = strip

        def trail(i, inner_carry):
            low = pl.multiple_of(i * BLOCK, BLOCK)
            side = held[pl.ds(at, BLOCK), pl.ds(low, BLOCK)]
            held[pl.ds(low, BLOCK), :] -= jnp.dot(
                side.T, held[pl.ds(at, BLOCK), :], precision=HIGHEST, preferred_element_type=jnp.float32
            )
            return inner_carry

        lax.fori_loop(k + 1, blocks, trail, 0)
        for i in range(4):
            @pl.when(k == min(i, blocks - 1))
            def _():
                stage(i)

        return carry

    lax.fori_loop(0, blocks, one, 0)
    inverse_out[...] = held[:size, padded : padded + size]
    arrive(spread(0))
    for j in range(wide):
        total[:, j * LANES : (j + 1) * LANES] = out[j * tall : (j + 1) * tall].reshape(size, LANES)
    for level in range(3):
        for sent in scatter(level) + spread(level):
            sent.wait_send()


def finish(sums, gram):
    n_row, n_col = lax.axis_size("row"), lax.axis_size("col")
    width = gram.shape[1]
    assert n_row % 2 == 0 and width % TILE == 0 and 2 * width % LANES == 0
    padded = -(-width // BLOCK) * BLOCK
    tiles = width * 2 * width // (TILE * LANES)
    tiles = -(-tiles // (n_row * n_col)) * n_row * n_col
    counts = [2, n_row // 2, n_col]
    dma = pltpu.SemaphoreType.DMA
    lands, sems, size = [], [], tiles
    for count in counts:
        size //= count
        lands.append(pltpu.VMEM((count - 1, size, TILE, LANES), jnp.float32))
        sems += [dma((count - 1,))] * 4
    vmem = pl.BlockSpec(memory_space=pltpu.VMEM)
    return pl.pallas_call(
        functools.partial(finish_kernel, n_row, n_col),
        out_shape=(jax.ShapeDtypeStruct((width, 2 * width), jnp.float32),
                   jax.ShapeDtypeStruct((width, width), jnp.float32)),
        in_specs=[vmem, vmem],
        out_specs=(vmem, vmem),
        scratch_shapes=[
            pltpu.VMEM((tiles, TILE, LANES), jnp.float32),
            pltpu.VMEM((tiles, TILE, LANES), jnp.float32),
            pltpu.VMEM((padded, 2 * padded), jnp.float32),
        ] + lands + sems,
        compiler_params=pltpu.CompilerParams(collective_id=1, has_side_effects=True),
    )(sums, gram)


def body(corner, edge, sketch):
    sums, gram = move(corner, edge, sketch.T)
    total, inverse = finish(sums, gram)
    width = gram.shape[1]
    inverse = inverse[width - RANK :]
    half = jnp.dot(inverse, total, precision=HIGHEST)

    def turn(side):
        return lax.dot_general(side, inverse, (((1,), (1,)), ((), ())), precision=HIGHEST)

    return turn(half[:, :width]), turn(half[:, width:])


def solution(mesh):
    placed = (P("row", "col"), P("row", "col"), P("col", None))
    return jax.shard_map(body, mesh=mesh, in_specs=placed, out_specs=(P(), P()), check_vma=False)
```

time: 338 us -> 231 us (0.68)
  Pallas kernels: 318 us -> 220 us
  local copies, waits for them, and re-layouts: 6.01 us -> 0.01 us
    pallas_call x3 -> x1, Pallas kernels: 170 us -> 57.2 us  [finish(): pl.pallas_call(functools.partial(finish_kernel, n_row, n_col), out_shape=...]
    pallas_call x1, Pallas kernels: 148 us -> 163 us  [move(): pl.pallas_call(functools.partial(move_kernel, n_row, n_col, shape), out_s...]
    slice x2 -> x0, local copies, waits for them, and re-layouts: 4.89 us -> none  [the longest x1 2.68 us: body(): return (result[:RANK], result[RANK:])]
    dot_general x5 -> x3, matrix products: 11.6 us -> 9.35 us  [the longest x2 4.82 us: turn(): lax.dot_general(side, inverse, (((1,), (1,)), ((), ())), precision=HIGHEST)]
where the time goes in v2:
time: 231 us; the launch traced here: 230 us
  Pallas kernels  220 us (95%)
  matrix products  9.35 us (4%)
    pallas_call x1, Pallas kernels, move(): pl.pallas_call(functools.partial(move_kernel, n_row, n_col, shape), out_s...  163 us
    pallas_call x1, Pallas kernels, finish(): pl.pallas_call(functools.partial(finish_kernel, n_row, n_col), out_shape=...  57.2 us
    dot_general x2, matrix products, turn(): lax.dot_general(side, inverse, (((1,), (1,)), ((), ())), precision=HIGHEST)  4.82 us

profile of v2, /device:TPU:31, one launch (start us, length us, event | category | flops | bytes accessed | tf_op | source)
XLA Modules:
  0.0 230.2 jit_solution(1093424025695332899)
XLA Ops:
  0.6 162.9 %shard_map.50 = (f32[448,896]{1,0:T(8,128)}, f32[512,448]{1,0:T(8,128)}) custom-call(bf16[6400,3200]{1,0:T(8,128)(2,1)} %corner.1, bf16[6400,3200]{1,0:T(8,128)(2,1)} %edge.1, bf16[448,3200]{1,0:T(8,128)(2,1)} %bitcast.2), custom_call_target="tpu_custom_call" | custom-call | tf_op jit(solution)/shard_map/pallas_call | solution.py:448
  163.6 57.2 %shard_map.51 = (f32[448,896]{1,0:T(8,128)}, f32[448,448]{1,0:T(8,128)}) custom-call(f32[448,896]{1,0:T(8,128)} %get-tuple-element.6.sums, f32[512,448]{1,0:T(8,128)} %get-tuple-element.7.gram), custom_call_target="tpu_custom_call" | custom-call | tf_op jit(solution)/shard_map/pallas_call | solution.py:664
  220.8 0.0 copy-start
  220.8 4.5 %fusion.6 = f32[400,896]{1,0:T(8,128)S(1)} fusion(f32[448,896]{1,0:T(8,128)} %get-tuple-element.9, f32[448,448]{1,0:T(8,128)} %get-tuple-element.8), kind=kOutput, calls=%fused_computation.6 | convolution fusion | flops 1926758400 | bytes 3858432 | tf_op jit(solution)/shard_map/dot_general | solution.py:684
  225.3 0.0 copy-done
  225.4 2.5 %fusion = f32[400,400]{1,0:T(8,128)} fusion(f32[400,896]{1,0:T(8,128)S(1)} %fusion.6, f32[448,448]{1,0:T(8,128)S(1)} %copy-done), kind=kOutput, calls=%fused_computation | convolution fusion | flops 860160000 | bytes 2278400 | tf_op jit(solution)/shard_map/dot_general | solution.py:687
  227.8 2.4 %fusion.2 = f32[400,400]{1,0:T(8,128)} fusion(f32[400,896]{1,0:T(8,128)S(1)} %fusion.6, f32[448,448]{1,0:T(8,128)S(1)} %copy-done), kind=kOutput, calls=%fused_computation.2 | convolution fusion | flops 860160000 | bytes 2278400 | tf_op jit(solution)/shard_map/dot_general | solution.py:687
Async XLA Ops:
  220.8 4.6 %copy-start = (f32[448,448]{1,0:T(8,128)S(1)}, f32[448,448]{1,0:T(8,128)}, u32[]{:S(2)}) copy-start(f32[448,448]{1,0:T(8,128)} %get-tuple-element.8) | copy-start | bytes 2408452

commit v3 on v2

--- a/solution.py
+++ b/solution.py
@@ -15,6 +15,8 @@
 SLOTS = 3
 AHEAD = 2
 VMEM_LIMIT = 67043328
+PROMPT = 12
+LATE = 6
 
 
 def across(left, right):
@@ -158,7 +160,6 @@
         greet(peer(d))
     for d in range(1, n_col):
         greet(column(d))
-    pl.semaphore_wait(barrier, n_row + n_col - 2)
 
     def gather(s):
         total = mine[:, span(s)].astype(jnp.float32)
@@ -203,7 +204,8 @@
             mine[:, span(s)] = tmp[...].astype(jnp.bfloat16)
             up_copy(s).start()
 
-    prompt = pieces - 10 if pieces > 10 else pieces
+    prompt = PROMPT if pieces > PROMPT else pieces
+    late = min(prompt + LATE, pieces)
 
     def hand_back(s):
         @pl.when(jnp.logical_not(owner))
@@ -284,6 +286,11 @@
                 mine[:, at] = found[0].astype(jnp.bfloat16)
                 for d in range(1, ratio):
                     away[d - 1, :, at] = found[d].astype(jnp.bfloat16)
+
+        @pl.when(t == 0)
+        def _():
+            pl.semaphore_wait(barrier, n_row + n_col - 2)
+
         for d in range(1, ratio):
             for i in range(per_tile):
                 near_copy(d, t * per_tile + i).start()
@@ -296,6 +303,26 @@
         start_at(total_sample + index)
     positions(0, early(tiles - 1), begin)
 
+    width, padded = cols.shape[0], square.shape[0]
+    big = padded // n_row
+    small = big // n_col
+
+    def at_rows(index, size):
+        return pl.ds(pl.multiple_of(index, TILE), size)
+
+    folds, pieces_out, fulls = [], [], []
+
+    def start_gram():
+        square[0:width, :] = across(cols[...], cols[...])
+        if padded > width:
+            square[width:padded, :] = jnp.zeros((padded - width, width), jnp.float32)
+        for d in range(1, n_col):
+            chunk_at = me_row * big + lax.rem(me_col + d, n_col) * small
+            folds.append(remote(square.at[at_rows(chunk_at, small), :], land.at[d - 1],
+                                fold_send.at[d - 1], fold_recv.at[d - 1], column(d)))
+            folds[-1].start()
+        swap(prompt, late)
+
     first = 0
     for g in range(n_groups):
         for i in range(groups[g]):
@@ -305,6 +332,8 @@
             def _():
                 cast_copy(1, s).wait_recv()
 
+        if g == n_groups - 1:
+            start_gram()
         every = parts[g] // tiles
 
         def image_tile(t, carry):
@@ -341,23 +370,25 @@
             positions(floor + first, begin + first + every * tiles, begin + first + parts[g])
         first += parts[g]
 
-    width, padded = cols.shape[0], square.shape[0]
-    big = padded // n_row
-    small = big // n_col
-
-    def at_rows(index, size):
-        return pl.ds(pl.multiple_of(index, TILE), size)
-
-    square[0:width, :] = across(cols[...], cols[...])
-    if padded > width:
-        square[width:padded, :] = jnp.zeros((padded - width, width), jnp.float32)
-    folds, pieces_out, fulls = [], [], []
-    for d in range(1, n_col):
-        chunk_at = me_row * big + lax.rem(me_col + d, n_col) * small
-        folds.append(remote(square.at[at_rows(chunk_at, small), :], land.at[d - 1],
-                            fold_send.at[d - 1], fold_recv.at[d - 1], column(d)))
-        folds[-1].start()
-    swap(prompt, min(prompt + 3, pieces))
+    sums[...] = jnp.zeros_like(sums)
+
+    def left(p, t):
+        images_t = jnp.concatenate([images[m, t, p] for m in range(2)], axis=0).astype(jnp.bfloat16)
+        sums[...] += across(rows[p, :, span(t * per_tile, per_tile)], images_t)
+
+    def own_tile(t, carry):
+        left(0, t)
+        return carry
+
+    def other_tile(t, carry):
+        for d in range(1, ratio):
+            for i in range(per_tile):
+                swap_copy(d, t * per_tile + i).wait_recv()
+        for p in range(1, ratio):
+            left(p, t)
+        return carry
+
+    lax.fori_loop(0, tiles, own_tile, 0)
     own = at_rows(me_row * big + me_col * small, small)
     summed = square[own, :]
     for d in range(1, n_col):
@@ -367,36 +398,18 @@
     for d in range(1, n_col):
         pieces_out.append(remote(piece, gram.at[own, :], part_send.at[d - 1], part_recv.at[d - 1], column(d)))
         pieces_out[-1].start()
-    swap(min(prompt + 3, pieces), pieces)
+    swap(late, pieces)
     gram[own, :] = summed
+    first_tiles = min(3, tiles)
+    lax.fori_loop(0, first_tiles, other_tile, 0)
     for d in range(1, n_col):
         pieces_out[d - 1].wait_recv()
     block = gram.at[at_rows(me_row * big, big), :]
     for d in range(1, n_row):
         fulls.append(remote(block, block, full_send.at[d - 1], full_recv.at[d - 1], peer(d)))
         fulls[-1].start()
-
-    sums[...] = jnp.zeros_like(sums)
-
-    def left_tile(t, carry):
-        for d in range(1, ratio):
-            for i in range(per_tile):
-                swap_copy(d, t * per_tile + i).wait_recv()
-        at = span(t * per_tile, per_tile)
-
-        def both(p):
-            return jnp.concatenate([images[m, t, p] for m in range(2)], axis=0).astype(jnp.bfloat16)
-
-        if chunk % LANES == 0:
-            left = jnp.concatenate([rows[p, :, at] for p in range(ratio)], axis=1)
-            right = jnp.concatenate([both(p) for p in range(ratio)], axis=1)
-            sums[...] += across(left, right)
-        else:
-            for p in range(ratio):
-                sums[...] += across(rows[p, :, at], both(p))
-        return carry
-
-    lax.fori_loop(0, tiles, left_tile, 0)
+    if first_tiles < tiles:
+        lax.fori_loop(first_tiles, tiles, other_tile, 0)
     for sent in fulls:
         sent.wait_recv()
     for sent in folds + pieces_out + fulls:
@@ -522,8 +535,9 @@
     return jnp.concatenate(done, axis=0)
 
 
-def finish_kernel(n_row, n_col, sums, gram, total, inverse_out, x, out, held, *rest):
-    lands, sems = rest[:3], rest[3:]
+def finish_kernel(n_row, n_col, shares, sums, gram, total, inverse_out, x, out, held, *rest):
+    orders = ((0, 1, 2), (0, 2, 1))
+    lands, sems = rest[:6], rest[6:]
     me_row, me_col = lax.axis_index("row"), lax.axis_index("col")
     inner, outer = lax.rem(me_row, 2), me_row // 2
     counts = [2, n_row // 2, n_col]
@@ -558,32 +572,52 @@
     held[:, padded:] = unit
     held[:size, :size] = gram[:size, :]
 
-    bases, sizes = [0], []
-    for level in range(3):
-        sizes.append((sizes[-1] if sizes else x.shape[0]) // counts[level])
-        bases.append(bases[-1] + mine[level] * sizes[-1])
-
-    def scatter(level):
-        m = sizes[level]
-        return [copy(x.at[pl.ds(bases[level] + lax.rem(mine[level] + d, counts[level]) * m, m)],
-                     lands[level].at[d - 1], sems[4 * level].at[d - 1], sems[4 * level + 1].at[d - 1], device(level, d))
-                for d in range(1, counts[level])]
-
-    def spread(level):
-        block = out.at[pl.ds(bases[level + 1], sizes[level])]
-        return [copy(block, block, sems[4 * level + 2].at[d - 1], sems[4 * level + 3].at[d - 1], device(level, d))
-                for d in range(1, counts[level])]
-
-    def fold(level):
-        own = pl.ds(bases[level + 1], sizes[level])
-        value = x[own]
-        for d, sent in enumerate(scatter(level)):
-            sent.wait_recv()
-            value += lands[level][d]
-        if level == 2:
-            out[own] = value
-        else:
-            x[own] = value
+    spots = []
+    for group, order in enumerate(orders):
+        base, size_now = shares[0] * group, shares[group]
+        steps = []
+        for level in order:
+            size_now //= counts[level]
+            steps.append((base, base + mine[level] * size_now, size_now))
+            base = base + mine[level] * size_now
+        spots.append(steps)
+
+    def links(group, step):
+        n = 3 * group + step
+        return lands[n], sems[4 * n : 4 * n + 4]
+
+    def scatter(step):
+        copies = []
+        for group, order in enumerate(orders):
+            level, (base, _, m) = order[step], spots[group][step]
+            land, (send, recv, _, _) = links(group, step)
+            copies += [copy(x.at[pl.ds(base + lax.rem(mine[level] + d, counts[level]) * m, m)],
+                            land.at[d - 1], send.at[d - 1], recv.at[d - 1], device(level, d))
+                       for d in range(1, counts[level])]
+        return copies
+
+    def spread(step):
+        copies = []
+        for group, order in enumerate(orders):
+            level, (_, at, m) = order[step], spots[group][step]
+            _, (_, _, send, recv) = links(group, step)
+            block = out.at[pl.ds(at, m)]
+            copies += [copy(block, block, send.at[d - 1], recv.at[d - 1], device(level, d))
+                       for d in range(1, counts[level])]
+        return copies
+
+    def fold(step):
+        arrive(scatter(step))
+        for group, order in enumerate(orders):
+            _, at, m = spots[group][step]
+            land, _ = links(group, step)
+            value = x[pl.ds(at, m)]
+            for d in range(counts[order[step]] - 1):
+                value += land[d]
+            if step == 2:
+                out[pl.ds(at, m)] = value
+            else:
+                x[pl.ds(at, m)] = value
 
     def begin(copies):
         for sent in copies:
@@ -652,17 +686,23 @@
     assert n_row % 2 == 0 and width % TILE == 0 and 2 * width % LANES == 0
     padded = -(-width // BLOCK) * BLOCK
     tiles = width * 2 * width // (TILE * LANES)
-    tiles = -(-tiles // (n_row * n_col)) * n_row * n_col
+    devices = n_row * n_col
+    units = -(-tiles // devices)
+    tiles = units * devices
+    less = max(1, units // 3)
+    shares = ((units - less) * devices, less * devices)
     counts = [2, n_row // 2, n_col]
     dma = pltpu.SemaphoreType.DMA
-    lands, sems, size = [], [], tiles
-    for count in counts:
-        size //= count
-        lands.append(pltpu.VMEM((count - 1, size, TILE, LANES), jnp.float32))
-        sems += [dma((count - 1,))] * 4
+    lands, sems = [], []
+    for share, order in zip(shares, ((0, 1, 2), (0, 2, 1))):
+        size = share
+        for level in order:
+            size //= counts[level]
+            lands.append(pltpu.VMEM((counts[level] - 1, size, TILE, LANES), jnp.float32))
+            sems += [dma((counts[level] - 1,))] * 4
     vmem = pl.BlockSpec(memory_space=pltpu.VMEM)
     return pl.pallas_call(
-        functools.partial(finish_kernel, n_row, n_col),
+        functools.partial(finish_kernel, n_row, n_col, shares),
         out_shape=(jax.ShapeDtypeStruct((width, 2 * width), jnp.float32),
                    jax.ShapeDtypeStruct((width, width), jnp.float32)),
         in_specs=[vmem, vmem],
@@ -681,10 +721,10 @@
     total, inverse = finish(sums, gram)
     width = gram.shape[1]
     inverse = inverse[width - RANK :]
-    half = jnp.dot(inverse, total, precision=HIGHEST)
+    half = jnp.dot(inverse, total, precision=lax.Precision.HIGH)
 
     def turn(side):
-        return lax.dot_general(side, inverse, (((1,), (1,)), ((), ())), precision=HIGHEST)
+        return lax.dot_general(side, inverse, (((1,), (1,)), ((), ())), precision=lax.Precision.HIGH)
 
     return turn(half[:, :width]), turn(half[:, width:])
 

time: 231 us -> 217 us (0.939)
  Pallas kernels: 220 us -> 209 us
  matrix products: 9.35 us -> 6.71 us
    pallas_call x1, Pallas kernels: 57.2 us -> 46.5 us  [finish(): pl.pallas_call(functools.partial(finish_kernel, n_row, n_col, shares), ou...]
    dot_general x3, matrix products: 9.35 us -> 6.71 us  [the longest x2 3.5 us: turn(): lax.dot_general(side, inverse, (((1,), (1,)), ((), ())), precision=lax.Pr...]
where the time goes in v3:
time: 217 us; the launch traced here: 216 us
  Pallas kernels  209 us (96%)
  matrix products  6.71 us (3%)
    pallas_call x1, Pallas kernels, move(): pl.pallas_call(functools.partial(move_kernel, n_row, n_col, shape), out_s...  162 us
    pallas_call x1, Pallas kernels, finish(): pl.pallas_call(functools.partial(finish_kernel, n_row, n_col, shares), ou...  46.5 us

profile of v3, /device:TPU:31, one launch (start us, length us, event | category | flops | bytes accessed | tf_op | source)
XLA Modules:
  0.0 216.1 jit_solution(16287174116482994523)
XLA Ops:
  0.6 162.3 %shard_map.50 = (f32[448,896]{1,0:T(8,128)}, f32[512,448]{1,0:T(8,128)}) custom-call(bf16[6400,3200]{1,0:T(8,128)(2,1)} %corner.1, bf16[6400,3200]{1,0:T(8,128)(2,1)} %edge.1, bf16[448,3200]{1,0:T(8,128)(2,1)} %bitcast.2), custom_call_target="tpu_custom_call" | custom-call | tf_op jit(solution)/shard_map/pallas_call | solution.py:461
  162.9 46.5 %shard_map.51 = (f32[448,896]{1,0:T(8,128)}, f32[448,448]{1,0:T(8,128)}) custom-call(f32[448,896]{1,0:T(8,128)} %get-tuple-element.6.sums, f32[512,448]{1,0:T(8,128)} %get-tuple-element.7.gram), custom_call_target="tpu_custom_call" | custom-call | tf_op jit(solution)/shard_map/pallas_call | solution.py:704
  209.4 0.0 copy-start
  209.4 3.2 %fusion.6 = f32[400,896]{1,0:T(8,128)S(1)} fusion(f32[448,896]{1,0:T(8,128)} %get-tuple-element.9, f32[448,448]{1,0:T(8,128)} %get-tuple-element.8), kind=kOutput, calls=%fused_computation.6 | convolution fusion | flops 963379200 | bytes 3858432 | tf_op jit(solution)/shard_map/dot_general | solution.py:724
  212.6 0.0 copy-done
  212.6 1.8 fusion
  214.4 1.7 fusion.2
Async XLA Ops:
  209.4 3.2 %copy-start = (f32[448,448]{1,0:T(8,128)S(1)}, f32[448,448]{1,0:T(8,128)}, u32[]{:S(2)}) copy-start(f32[448,448]{1,0:T(8,128)} %get-tuple-element.8) | copy-start | bytes 2408452

commit v4 on v3

--- a/solution.py
+++ b/solution.py
@@ -41,7 +41,7 @@
     for g in range(2, len(groups)):
         parts.append(total // (len(groups) - g))
         total -= parts[-1]
-    return sub, pieces, 5, groups, lead, parts, lag, stride, pieces - 3
+    return sub, pieces, 5, groups, lead, parts, lag, stride, pieces - 7
 
 
 def move_kernel(n_row, n_col, shape, corner, edge, sketch, sums, gram, cols, ring, images, mine, away, near, upper, lower, rows, scratch, square, land, piece, *sems):

time: 217 us -> 209 us (0.963)
  Pallas kernels: 209 us -> 201 us
    pallas_call x1, Pallas kernels: 162 us -> 158 us  [move(): pl.pallas_call(functools.partial(move_kernel, n_row, n_col, shape), out_s...]
    pallas_call x1, Pallas kernels: 46.5 us -> 43.8 us  [finish(): pl.pallas_call(functools.partial(finish_kernel, n_row, n_col, shares), ou...]
where the time goes in v4:
time: 209 us
  Pallas kernels  201 us (96%)
  matrix products  6.71 us (3%)
    pallas_call x1, Pallas kernels, move(): pl.pallas_call(functools.partial(move_kernel, n_row, n_col, shape), out_s...  158 us
    pallas_call x1, Pallas kernels, finish(): pl.pallas_call(functools.partial(finish_kernel, n_row, n_col, shares), ou...  43.8 us

profile of v4, /device:TPU:31, one launch (start us, length us, event | category | flops | bytes accessed | tf_op | source)
XLA Modules:
  0.0 208.7 jit_solution(16210388958950705499)
XLA Ops:
  0.6 157.6 %shard_map.50 = (f32[448,896]{1,0:T(8,128)}, f32[512,448]{1,0:T(8,128)}) custom-call(bf16[6400,3200]{1,0:T(8,128)(2,1)} %corner.1, bf16[6400,3200]{1,0:T(8,128)(2,1)} %edge.1, bf16[448,3200]{1,0:T(8,128)(2,1)} %bitcast.2), custom_call_target="tpu_custom_call" | custom-call | tf_op jit(solution)/shard_map/pallas_call | solution.py:461
  158.2 43.8 %shard_map.51 = (f32[448,896]{1,0:T(8,128)}, f32[448,448]{1,0:T(8,128)}) custom-call(f32[448,896]{1,0:T(8,128)} %get-tuple-element.6.sums, f32[512,448]{1,0:T(8,128)} %get-tuple-element.7.gram), custom_call_target="tpu_custom_call" | custom-call | tf_op jit(solution)/shard_map/pallas_call | solution.py:704
  202.0 0.0 copy-start
  202.0 3.2 %fusion.6 = f32[400,896]{1,0:T(8,128)S(1)} fusion(f32[448,896]{1,0:T(8,128)} %get-tuple-element.9, f32[448,448]{1,0:T(8,128)} %get-tuple-element.8), kind=kOutput, calls=%fused_computation.6 | convolution fusion | flops 963379200 | bytes 3858432 | tf_op jit(solution)/shard_map/dot_general | solution.py:724
  205.2 0.0 copy-done
  205.2 1.8 fusion
  207.0 1.7 fusion.2
Async XLA Ops:
  202.0 3.2 %copy-start = (f32[448,448]{1,0:T(8,128)S(1)}, f32[448,448]{1,0:T(8,128)}, u32[]{:S(2)}) copy-start(f32[448,448]{1,0:T(8,128)} %get-tuple-element.8) | copy-start | bytes 2408452
